TPU v7x, 256 devices: a whole 4x4x8 slice. The times are simulated.
256 devices in a mesh: grp: 16 (over y, z_lo), blk: 16 (over x, z_hi, core).
Axes of the slice: x: 4, y: 4, z: 8 (z_hi: 2, z_lo: 4; z = z_hi * 4 + z_lo), core: 2. Of those that a mesh axis runs over, the one named last changes fastest.
Arguments:
- front_values: float32 [16384, 16384], P('blk', 'grp'), may hold values from -6 to 6
- diag_scale: float32 [16384], P('blk'), may hold values from 1.5 to 3
- fill_pattern: int32 [128, 128], P('blk', 'grp'), may hold values from 0 to 1, as said below
- supernodes: int32 [2], replicated, may hold values from 0 to 126, as said below
- scenario_loads: float32 [512, 16384], P(('grp', 'blk')), may hold values from -6 to 6
Outputs:
- factored: float32 [16384, 16384], P('blk', 'grp')
- forward_rhs: float32 [512, 16384], P('grp', 'blk')
Inputs may be any that keep to these rules, and one draw needn't show every extreme that they name: `fill_pattern`: each entry is 0 or 1; every diagonal block is 1. `supernodes`: two different multiples of 2; the second is always 128 - 2, the last supernode.
All inputs are finite; a program needn't handle non-finite values.
Results may differ from a plain program's by a relative error of at most 0.0001.
Values sent between devices are 32-bit elements; how exact they have to be, the bound alone decides.
A program may use at most 64 MiB of HBM per device.

v0:
```python
import math

import jax
import jax.numpy as jnp
from jax import lax
from jax.sharding import PartitionSpec as P

BS = 128
SNB = 2
NS_STEPS = 3


HIGH = lax.Precision.HIGHEST


def broadcast(value, axis, source):
    kept = jnp.where(lax.axis_index(axis) == source, value, 0).astype(value.dtype)
    return lax.psum(kept, axis)


def newton_inverse(pivot):
    inverse = jnp.diag(1.0 / jnp.diagonal(pivot))
    for sweep in range(NS_STEPS):
        product = jnp.dot(pivot, inverse, precision=HIGH)
        inverse = 2.0 * inverse - jnp.dot(inverse, product, precision=HIGH)
    return inverse


def per_device(front_values, diag_scale, fill_pattern, supernodes, scenario_loads):
    local_rows, local_cols = front_values.shape
    width = SNB * BS
    blk_index = lax.axis_index("blk")
    grp_index = lax.axis_index("grp")
    order_total = local_rows * lax.axis_size("blk")
    row_ids = blk_index * local_rows + jnp.arange(local_rows, dtype=jnp.int32)
    col_ids = grp_index * local_cols + jnp.arange(local_cols, dtype=jnp.int32)
    present = jnp.repeat(jnp.repeat(fill_pattern > 0, BS, axis=0), BS, axis=1)
    shifted = diag_scale * math.sqrt(order_total)
    front = jnp.where(present, front_values, jnp.float32(0.0))
    front = front + jnp.where(
        row_ids[:, None] == col_ids[None, :], shifted[:, None], jnp.float32(0.0)
    )
    rhs = lax.all_to_all(scenario_loads, "blk", split_axis=1, concat_axis=0, tiled=True)
    row_blocks = row_ids // BS
    col_blocks = col_ids // BS
    row_alive = jnp.ones((local_rows,), dtype=bool)
    col_alive = jnp.ones((local_cols,), dtype=bool)
    for step in range(2):
        first_block = supernodes[step]
        start = first_block * BS
        row_alive = row_alive & ~((row_blocks >= first_block) & (row_blocks < first_block + SNB))
        col_alive = col_alive & ~((col_blocks >= first_block) & (col_blocks < first_block + SNB))
        row_root = start // local_rows
        col_root = start // local_cols
        row_offset = start - blk_index * local_rows
        col_offset = start - grp_index * local_cols
        rows_mine = lax.dynamic_slice_in_dim(front, row_offset, width, 0)
        rhs_mine = lax.dynamic_slice_in_dim(rhs, row_offset, width, 1)
        pivot_rows, pivot_rhs = (
            broadcast(rows_mine, "blk", row_root),
            broadcast(rhs_mine, "blk", row_root),
        )
        cols_mine = lax.dynamic_slice_in_dim(front, col_offset, width, 1)
        block_mine = lax.dynamic_slice_in_dim(pivot_rows, col_offset, width, 1)
        pivot_block = broadcast(block_mine, "grp", col_root)
        panel_cols = broadcast(cols_mine, "grp", col_root)
        panel = jnp.dot(panel_cols, newton_inverse(pivot_block), precision=HIGH)
        lower = jnp.where(row_alive[:, None], panel, jnp.float32(0.0))
        written = lax.dynamic_update_slice_in_dim(
            front, jnp.where(row_alive[:, None], panel, cols_mine), col_offset, 1
        )
        front = jnp.where(grp_index == col_root, written, front)
        upper = jnp.where(col_alive[None, :], pivot_rows, jnp.float32(0.0))
        front = front - jnp.dot(lower, upper, precision=HIGH)
        rhs = rhs - lax.dot_general(pivot_rhs, lower, (((1,), (1,)), ((), ())), precision=HIGH)
    return (front, rhs)


def solution(mesh):
    in_specs = (P("blk", "grp"), P("blk"), P("blk", "grp"), P(), P(("grp", "blk"), None))
    out_specs = (P("blk", "grp"), P("grp", "blk"))
    return jax.shard_map(
        per_device, mesh=mesh, in_specs=in_specs, out_specs=out_specs, check_vma=False
    )
```

profile of v0, /device:TPU:1, one launch (start us, length us, event | category | flops | bytes accessed | tf_op | source)
XLA Modules:
  0.0 779.8 jit_solution(8850190974641949622)
XLA Ops:
  10.5 3.2 broadcast_in_dim.120
  13.7 2.9 select_add_fusion
  16.6 2.0 copy-done
  19.7 2.3 dynamic-slice_select_fusion.3
  22.1 183.0 %all-reduce.7.cloned.1.call-done = f32[256,1024]{1,0:T(8,128)} async-done(((f32[256,1024]{1,0:T(8,128)}), f32[256,1024]{1,0:T(8,128)}) %all-reduce.7.cloned.1.call-update) | async-done | bytes 1048592 | tf_op jit(solution)/shard_map/psum | solution.py:18
  205.0 1.7 dynamic-slice_select_fusion.5
  209.1 157.7 %all-reduce.13.cloned.1.call-done = (f32[1024,256]{1,0:T(8,128)}, f32[256,256]{1,0:T(8,128)}) async-done(((f32[1024,256]{1,0:T(8,128)}, f32[256,256]{1,0:T(8,128)}), (f32[1024,256]{1,0:T(8,128)}, f32[256,256]{1,0:T(8,128)})) %all-reduce.13.cloned.1.call-update) | async-done | bytes 1310736 | tf_op jit(solution)/shard_map/psum | solution.py:18
  366.9 2.7 gather_fusion
  369.5 1.6 fusion.24
  371.5 1.3 fusion.49
  376.0 3.8 convolution_subtract_fusion.1
  379.9 2.0 copy-done.2
  383.0 2.3 dynamic-slice_select_fusion.2
  385.3 187.5 %all-reduce.9.cloned.1.call-done = f32[256,1024]{1,0:T(8,128)} async-done(((f32[256,1024]{1,0:T(8,128)}), f32[256,1024]{1,0:T(8,128)}) %all-reduce.9.cloned.1.call-update) | async-done | bytes 1048592 | tf_op jit(solution)/shard_map/psum | solution.py:18
  572.8 1.7 dynamic-slice_select_fusion.4
  574.5 9.7 %all-to-all-start = ((f32[2,16,1024]{2,0,1:T(2,128)}), f32[2,16,1024]{2,0,1:T(2,128)S(1)}, u32[]{:S(2)}, u32[]{:S(2)}) async-start(f32[2,16,1024]{2,0,1:T(2,128)} %bitcast.4), calls=%async_computation | async-start | bytes 262144 | tf_op jit(solution)/shard_map/all_to_all | solution.py:43
  587.3 6.9 all-to-all-done
  594.4 77.2 %psum.62 = f32[32,256]{1,0:T(8,128)S(1)} all-reduce(f32[32,256]{1,0:T(8,128)S(1)} %dynamic-slice_select_fusion.7), channel_id=1, replica_groups=mesh['grp'=16,'blk'=16] {'blk'}, use_global_device_ids=true, to_apply=%region_6.7 | all-reduce | flops 8192 | bytes 65536 | tf_op jit(solution)/shard_map/psum | solution.py:18
  672.8 84.2 %psum.63 = f32[32,256]{1,0:T(8,128)S(1)} all-reduce(f32[32,256]{1,0:T(8,128)S(1)} %dynamic-slice_select_fusion.6), channel_id=1, replica_groups=mesh['grp'=16,'blk'=16] {'blk'}, use_global_device_ids=true, to_apply=%region_7.8 | all-reduce | flops 8192 | bytes 65536 | tf_op jit(solution)/shard_map/psum | solution.py:18
  757.1 2.7 gather_fusion.1
  759.7 1.6 fusion.21
  763.4 1.3 fusion.52
  766.2 1.8 convolution_subtract_fusion.8
  768.0 5.2 convolution_subtract_fusion
  (51 shorter events, 17.0 us)
Async XLA Ops:
  7.2 197.9 %all-reduce.7.cloned.1.call-start = ((), (), s32[]{:S(2)}) async-start(), calls=%async_computation.1 | async-start | bytes 2097152 | tf_op jit(solution)/shard_map/psum | solution.py:18
  16.6 2.0 copy-start
  19.7 347.2 %all-reduce.13.cloned.1.call-start = ((), (), s32[]{:S(2)}) async-start(), calls=%async_computation.4 | async-start | bytes 2621440 | tf_op jit(solution)/shard_map/psum | solution.py:18
  206.7 366.1 %all-reduce.9.cloned.1.call-start = ((), (), s32[]{:S(2)}) async-start(), calls=%async_computation.2 | async-start | bytes 2097152 | tf_op jit(solution)/shard_map/psum | solution.py:18
  366.9 8.1 %copy-start.6 = (f32[1024,256]{1,0:T(8,128)S(1)}, f32[1024,256]{1,0:T(8,128)}, u32[]{:S(2)}) copy-start(f32[1024,256]{1,0:T(8,128)} %get-tuple-element.4) | copy-start | bytes 3145732
  369.5 5.5 copy-start.1
  371.1 4.9 copy-start.4
  379.9 2.0 copy-start.2
  383.0 374.1 %all-reduce.11.cloned.1.call-start = ((), (), s32[]{:S(2)}) async-start(), calls=%async_computation.3 | async-start | bytes 2621440 | tf_op jit(solution)/shard_map/psum | solution.py:18
  574.5 19.8 %all-to-all-start = ((f32[2,16,1024]{2,0,1:T(2,128)}), f32[2,16,1024]{2,0,1:T(2,128)S(1)}, u32[]{:S(2)}, u32[]{:S(2)}) async-start(f32[2,16,1024]{2,0,1:T(2,128)} %bitcast.4), calls=%async_computation | async-start | bytes 262144 | tf_op jit(solution)/shard_map/all_to_all | solution.py:43
  757.1 8.1 %copy-start.7 = (f32[1024,256]{1,0:T(8,128)S(1)}, f32[1024,256]{1,0:T(8,128)}, u32[]{:S(2)}) copy-start(f32[1024,256]{1,0:T(8,128)} %get-tuple-element.2) | copy-start | bytes 3145732
  759.7 5.5 copy-start.3
  763.0 5.0 copy-start.5
Sparse Core Ops, SparseCore 0:
  19.8 185.1 all-reduce.6
  207.7 159.0 all-reduce.12
  383.1 189.6 all-reduce.8
  575.4 159.4 all-reduce.10
where the time goes:
time: 788 us; the launch traced here: 780 us
  waiting for transfers between devices  535 us (68%)
  blocking collectives  161 us (20%)
  matrix products  24.8 us (3%)
  other arithmetic  17.9 us (2%)
  between operations  16.5 us (2%)
  local copies, waits for them, and re-layouts  14 us (2%)
  starting transfers between devices  9.9 us (1%)
    psum x4, waiting for transfers between devices, broadcast(): return lax.psum(kept, axis)  528 us
    psum x2, blocking collectives, broadcast(): return lax.psum(kept, axis)  161 us
  transfers between devices with their start and end apart: 5, of which 4 were waited for; matrix products, arithmetic and copies ran while one was open for 1% of the time, Pallas kernels for 0%

commit v1 on v0

v1 whole, which is shorter than its diff:
```python
import functools
import math

import jax
import jax.numpy as jnp
from jax import lax
from jax.experimental import pallas as pl
from jax.experimental.pallas import tpu as pltpu
from jax.sharding import PartitionSpec as P

MESH = pl.DeviceIdType.MESH
HIGH = lax.Precision.HIGHEST
F32 = jnp.float32
BF16 = jnp.bfloat16

BS = 128
W = 256
NS_STEPS = 3
CH = 16
N = 256 // CH
L = 2
NR = 4
COFF = (0, 1, 1, 2)
SIGN = (1, 1, 3, 3)
LAST = 15


def quarter_of(u, s0, b):
    r0, q0 = s0 // 8, (s0 % 8) // 2
    first = jnp.where(b == r0, q0, jnp.where(b == LAST, 3, 0))
    both = (b == r0) & (b == LAST)

    def swap(v):
        return jnp.where(v == 0, first, jnp.where(v == first, 0, v))

    v = jnp.where(both & (u == 1), 3, jnp.where(both & (u == 3), 1, u))
    return swap(v)


def masked(values, rows, cols, row0, col0, fill_ref, shift, on_diag):
    out = []
    for i in range(rows):
        line = []
        for j in range(cols):
            v = values[i * BS : (i + 1) * BS, j * BS : (j + 1) * BS]
            v = jnp.where(fill_ref[row0 + i, col0 + j] > 0, v, 0.0)
            same = on_diag & (row0 + i == col0 + j)
            r = lax.broadcasted_iota(jnp.int32, (BS, BS), 0)
            c = lax.broadcasted_iota(jnp.int32, (BS, BS), 1)
            d = shift[pl.ds(row0 + i, 1), :]
            v = v + jnp.where((r == c) & same, d, 0.0)
            line.append(v)
        out.append(jnp.concatenate(line, axis=1) if cols > 1 else line[0])
    return jnp.concatenate(out, axis=0) if rows > 1 else out[0]


def prep_kernel(sc, fill, front, top0, top1, shift, loads, cbuf, rbuf, piv):
    u = pl.program_id(0)
    s0, g, b = sc[0], sc[2], sc[3]
    q0 = (s0 % 8) // 2
    aq = quarter_of(u, s0, b)
    diag = g == b
    for k, q in ((0, q0), (1, 3)):
        v = front[:, pl.ds(pl.multiple_of(q * W, W), W)]
        v = masked(v, 2, 2, aq * 2, q * 2, fill, shift, diag)
        cbuf[k] = v.reshape(4, 64, W)
        t = (top0, top1)[k][...]
        rbuf[k] = masked(t, 2, 2, q * 2, u * 2, fill, shift, diag)
    piv[:, 0:W] = loads[:, pl.ds(pl.multiple_of(s0 * BS, W), W)]
    piv[:, W : 2 * W] = loads[:, loads.shape[1] - W :]


def comm_kernel(r0, cin, rin, loads, piv, cbuf, rbuf, dbuf, hbuf, pbuf,
                cs, cr, rs, rown, roth, dsem, down, doth, hs, hr, loc):
    g, b = lax.axis_index("grp"), lax.axis_index("blk")
    y, zl = g // 4, g % 4
    x, zh, c = b // 4, (b // 2) % 2, b % 2
    partner = {"blk": x * 4 + zh * 2 + (1 - c)}

    barrier = pltpu.get_barrier_semaphore()

    @pl.loop(1, 16)
    def _(i):
        pl.semaphore_signal(barrier, inc=1, device_id={"blk": (b + i) % 16}, device_id_type=MESH)

    for t in (((y + 1) % 4) * 4 + zl, ((y + 3) % 4) * 4 + zl, y * 4 + (zl + 1) % 4, y * 4 + (zl + 3) % 4):
        pl.semaphore_signal(barrier, inc=1, device_id={"grp": t}, device_id_type=MESH)
    pl.semaphore_wait(barrier, 19)

    def rdma(src, dst, ssem, rsem, to):
        return pltpu.make_async_remote_copy(
            src_ref=src, dst_ref=dst, send_sem=ssem, recv_sem=rsem, device_id=to, device_id_type=MESH)

    roots = (r0, LAST)
    place = (0, 1 if r0 == LAST else 0)

    cplan = []
    for k in range(2):
        yk, zk = roots[k] // 4, roots[k] % 4
        inplane = zl == zk
        e = jnp.where(zl > zk, zl - zk, zk - zl)
        for cls in range(4):
            a = ((y + 4 - yk) * SIGN[cls]) % 4
            eff = jnp.where(inplane, a, (a + 4 - COFF[cls]) % 4)
            lag = jnp.where(inplane, a, COFF[cls] + e + eff) * L
            at = a == COFF[cls]
            cplan.append(dict(
                k=k, cls=cls, lag=lag, root=inplane & (a == 0), ring=eff != 3,
                up=at & (zl >= zk) & (zl < 3), dn=at & (zl <= zk) & (zl > 0),
                ringto={"grp": ((y + SIGN[cls]) % 4) * 4 + zl},
                upto={"grp": y * 4 + jnp.minimum(zl + 1, 3)}, dnto={"grp": y * 4 + jnp.maximum(zl - 1, 0)}))
    rplan = []
    for k in range(2):
        xk, hk, ck = roots[k] // 4, (roots[k] // 2) % 2, roots[k] % 2
        inhalf = zh == hk
        for cls in range(4):
            a = ((x + 4 - xk) * SIGN[cls]) % 4
            eff = jnp.where(inhalf, a, (a + 4 - COFF[cls]) % 4)
            lag = jnp.where(inhalf, a, COFF[cls] + 2 + eff) * L + jnp.where(c == ck, 0, L)
            chip = inhalf & (x == xk)
            rplan.append(dict(
                k=k, cls=cls, lag=lag, root=chip & (c == ck), mate=chip & (c != ck), ring=eff != 3,
                cross=inhalf & (a == COFF[cls]),
                ringto={"blk": ((x + SIGN[cls]) % 4) * 4 + zh * 2 + c},
                crossto={"blk": x * 4 + (1 - zh) * 2 + c}))
    tds = [(place[k] + 1) * (64 // CH) + 8 * L for k in range(2)]
    turns = max(N + 8 * L, max(tds) + 2 + 9 * L)

    @pl.loop(1, 16)
    def _(i):
        to = (b + i) % 16
        cols = pl.ds(pl.multiple_of(to * 1024, 1024), 1024)
        rdma(loads.at[:, cols], hbuf.at[b], hs.at[0], hr.at[0, i], {"blk": to}).start()
        rdma(piv, pbuf.at[b], hs.at[1], hr.at[1, i], {"blk": to}).start()

    mine = [
        pltpu.make_async_copy(loads.at[:, pl.ds(pl.multiple_of(b * 1024, 1024), 1024)], hbuf.at[b], loc.at[0]),
        pltpu.make_async_copy(piv, pbuf.at[b], loc.at[1]),
    ]
    for m in mine:
        m.start()

    def dlocal(k):
        lo = place[k] * 64
        return pltpu.make_async_copy(cbuf.at[:, :, pl.ds(lo, 64), :], dbuf.at[k], loc.at[2 + k])

    @pl.loop(0, turns)
    def _(t):
        for p in cplan:
            k, cls = p["k"], p["cls"]
            n = t - p["lag"]

            @pl.when((n >= 0) & (n < N))
            def _():
                rows = cbuf.at[k, cls, pl.ds(pl.multiple_of(n * CH, CH), CH), :]
                sem = cr.at[k, cls, n]

                @pl.when(jnp.logical_not(p["root"]))
                def _():
                    rdma(rows, rows, cs.at[0, k, cls], sem, p["ringto"]).wait_recv()

                for i, (on, to) in enumerate((("ring", "ringto"), ("up", "upto"), ("dn", "dnto"))):
                    @pl.when(p[on])
                    def _():
                        rdma(rows, rows, cs.at[i, k, cls], sem, p[to]).start()

        for p in rplan:
            k, cls = p["k"], p["cls"]
            n = t - p["lag"]

            @pl.when((n >= 0) & (n < NR))
            def _():
                rows = rbuf.at[k, c, cls, pl.ds(pl.multiple_of(n * 8, 8), 8), :]

                @pl.when(jnp.logical_not(p["root"]))
                def _():
                    rdma(rows, rows, rs.at[0, k, cls], rown.at[k, cls, n], p["ringto"]).wait_recv()

                for i, (on, to) in enumerate((("ring", "ringto"), ("cross", "crossto"))):
                    @pl.when(p[on])
                    def _():
                        rdma(rows, rows, rs.at[i, k, cls], rown.at[k, cls, n], p[to]).start()

                @pl.when(jnp.logical_not(p["mate"]))
                def _():
                    rdma(rows, rows, rs.at[2, k, cls], roth.at[k, cls, n], partner).start()

                @pl.when(p["root"])
                def _():
                    other = rbuf.at[k, 1 - c, cls, pl.ds(pl.multiple_of(n * 8, 8), 8), :]
                    rdma(other, other, rs.at[3, k, cls], rown.at[k, cls, n], partner).start()

            j = n - tds[k]

            @pl.when((j >= 0) & (j < 2))
            def _():
                part = pl.ds(pl.multiple_of(c * 32, 32), 32)
                dst = dbuf.at[k, j, cls, part, :]
                sem = down.at[k, cls, j]

                @pl.when(p["root"])
                def _():
                    lo = place[k] * 64
                    src = cbuf.at[j, cls, pl.ds(pl.multiple_of(lo + c * 32, 32), 32), :]
                    for i, (on, to) in enumerate((("ring", "ringto"), ("cross", "crossto"))):
                        @pl.when(p[on])
                        def _():
                            rdma(src, dst, dsem.at[i, k, cls], sem, p[to]).start()

                    rdma(src, dst, dsem.at[2, k, cls], doth.at[k, cls, j], partner).start()
                    src2 = cbuf.at[j, cls, pl.ds(pl.multiple_of(lo + (1 - c) * 32, 32), 32), :]
                    dst2 = dbuf.at[k, j, cls, pl.ds(pl.multiple_of((1 - c) * 32, 32), 32), :]
                    rdma(src2, dst2, dsem.at[3, k, cls], sem, partner).start()

                @pl.when(jnp.logical_not(p["root"]))
                def _():
                    rdma(dst, dst, dsem.at[0, k, cls], sem, p["ringto"]).wait_recv()
                    for i, (on, to) in enumerate((("ring", "ringto"), ("cross", "crossto"))):
                        @pl.when(p[on])
                        def _():
                            rdma(dst, dst, dsem.at[i, k, cls], sem, p[to]).start()

                    @pl.when(jnp.logical_not(p["mate"]))
                    def _():
                        rdma(dst, dst, dsem.at[2, k, cls], doth.at[k, cls, j], partner).start()

        for k in range(2):
            @pl.when((t == tds[k]) & (b == roots[k]))
            def _():
                dlocal(k).start()

    for p in rplan:
        k, cls = p["k"], p["cls"]

        @pl.when(jnp.logical_not(p["root"]))
        def _():
            @pl.loop(0, NR)
            def _(n):
                rows = rbuf.at[k, 1 - c, cls, pl.ds(pl.multiple_of(n * 8, 8), 8), :]
                rdma(rows, rows, rs.at[2, k, cls], roth.at[k, cls, n], partner).wait_recv()

            @pl.loop(0, 2)
            def _(j):
                rows = dbuf.at[k, j, cls, pl.ds(pl.multiple_of((1 - c) * 32, 32), 32), :]
                rdma(rows, rows, dsem.at[2, k, cls], doth.at[k, cls, j], partner).wait_recv()

    @pl.loop(1, 16)
    def _(i):
        rdma(piv, pbuf.at[b], hs.at[1], hr.at[1, i], partner).wait_recv()
        rdma(hbuf.at[b], hbuf.at[b], hs.at[0], hr.at[0, i], partner).wait_recv()

    for p in cplan:
        k, cls = p["k"], p["cls"]
        for i, on in enumerate(("ring", "up", "dn")):
            @pl.when(p[on])
            def _():
                rdma(cbuf.at[k, cls], cbuf.at[k, cls], cs.at[i, k, cls], cr.at[k, cls, 0], p["ringto"]).wait_send()
    for p in rplan:
        k, cls = p["k"], p["cls"]
        half = rbuf.at[k, c, cls]
        dhalf = dbuf.at[k, :, cls, pl.ds(pl.multiple_of(c * 32, 32), 32), :]
        for i, on in enumerate((p["ring"], p["cross"], jnp.logical_not(p["mate"]), p["root"])):
            @pl.when(on)
            def _():
                rdma(half, half, rs.at[i, k, cls], rown.at[k, cls, 0], p["ringto"]).wait_send()
                rdma(dhalf, dhalf, dsem.at[i, k, cls], down.at[k, cls, 0], p["ringto"]).wait_send()
    for m in mine:
        m.wait()
    for k in range(2):
        @pl.when(b == roots[k])
        def _():
            dlocal(k).wait()

    @pl.loop(1, 16)
    def _(i):
        rdma(hbuf.at[b], hbuf.at[b], hs.at[0], hr.at[0, i], partner).wait_send()
        rdma(piv, pbuf.at[b], hs.at[1], hr.at[1, i], partner).wait_send()


def comm(r0, cbuf, rbuf, loads, piv):
    anyspec = pl.BlockSpec(memory_space=pl.ANY)
    dma = pltpu.SemaphoreType.DMA
    return pl.pallas_call(
        functools.partial(comm_kernel, r0),
        out_shape=(
            jax.ShapeDtypeStruct(cbuf.shape, F32),
            jax.ShapeDtypeStruct(rbuf.shape, F32),
            jax.ShapeDtypeStruct((2, 2, 4, 64, W), F32),
            jax.ShapeDtypeStruct((16, 2, 1024), F32),
            jax.ShapeDtypeStruct((16, 2, 2 * W), F32),
        ),
        in_specs=[anyspec] * 4,
        out_specs=(anyspec,) * 5,
        input_output_aliases={0: 0, 1: 1},
        scratch_shapes=[
            dma((3, 2, 4)), dma((2, 4, N)),
            dma((4, 2, 4)), dma((2, 4, NR)), dma((2, 4, NR)),
            dma((4, 2, 4)), dma((2, 4, 2)), dma((2, 4, 2)),
            dma((2,)), dma((2, 16)), dma((4,)),
        ],
        compiler_params=pltpu.CompilerParams(collective_id=r0, has_side_effects=True),
        name="exchange_%d" % r0,
    )(cbuf, rbuf, loads, piv)


def split(v):
    hi = v.astype(BF16)
    return hi, (v - hi.astype(F32)).astype(BF16)


def mm(a, b):
    return jnp.dot(a, b, preferred_element_type=F32)


def mm3(a, b):
    return mm(a[0], b[0]) + (mm(a[0], b[1]) + mm(a[1], b[0]))


def mm3t(a, b):
    dims = (((1,), (1,)), ((), ()))

    def one(p, q):
        return lax.dot_general(p, q, dims, preferred_element_type=F32)

    return one(a[0], b[0]) + (one(a[0], b[1]) + one(a[1], b[0]))


def full(a, b):
    return jnp.dot(a, b, precision=HIGH, preferred_element_type=F32)


def newton(pivot):
    n = pivot.shape[0]
    r = lax.broadcasted_iota(jnp.int32, (n, n), 0)
    c = lax.broadcasted_iota(jnp.int32, (n, n), 1)
    eye = r == c
    kept = jnp.where(eye, pivot, 0.0)
    drow = 1.0 / jnp.sum(kept, axis=0, keepdims=True)
    dcol = 1.0 / jnp.sum(kept, axis=1, keepdims=True)
    inv = jnp.where(eye, 2.0 * drow, 0.0) - dcol * (pivot * drow)
    for _ in range(NS_STEPS - 1):
        inv = 2.0 * inv - full(inv, full(pivot, inv))
    return inv


def update_kernel(sc, fill, front, shift, cbuf, rbuf, dbuf, hbuf, pbuf, out, hout,
                  x0h, x0l, x1h, x1l, d1h, d1l, uh, ul, pvh, pvl):
    u = pl.program_id(0)
    s0, g, b = sc[0], sc[2], sc[3]
    r0, q0 = s0 // 8, (s0 % 8) // 2
    cols = front.shape[1]
    ids = lax.broadcasted_iota(jnp.int32, (1, cols), 1) // W
    dead0 = (g == r0) & (ids == q0)
    dead1 = (g == LAST) & (ids == 3)

    @pl.when(u == 0)
    def _():
        d = [[dbuf[i, j].reshape(W, W) for j in range(2)] for i in range(2)]
        x0 = newton(d[0][0])
        m = full(d[1][0], x0)
        x1 = newton(d[1][1] - full(m, d[0][1]))
        x0h[...], x0l[...] = split(x0)
        x1h[...], x1l[...] = split(x1)
        d1h[...], d1l[...] = split(d[0][1])
        ms = split(m)
        u0 = jnp.where(dead0, 0.0, rbuf[0])
        u0s = split(u0)
        u1 = jnp.where(dead0 | dead1, 0.0, rbuf[1] - mm3(ms, u0s))
        u1s = split(u1)
        uh[0:W], ul[0:W] = u0s
        uh[W : 2 * W], ul[W : 2 * W] = u1s
        pv = jnp.concatenate([pbuf[:, 0, :], pbuf[:, 1, :]], axis=0)
        p0 = split(pv[:, 0:W])
        p1 = split(pv[:, W : 2 * W] - mm3t(p0, ms))
        pvh[:, 0:W], pvl[:, 0:W] = p0
        pvh[:, W : 2 * W], pvl[:, W : 2 * W] = p1

    aq = quarter_of(u, s0, b)
    gone0 = (b == r0) & (aq == q0)
    gone1 = (b == LAST) & (aq == 3)
    c0 = cbuf[0].reshape(W, W)
    l0 = mm3(split(c0), (x0h[...], x0l[...]))
    l0 = jnp.where(gone0, 0.0, l0)
    l0s = split(l0)
    c1 = cbuf[1].reshape(W, W) - mm3(l0s, (d1h[...], d1l[...]))
    l1 = mm3(split(c1), (x1h[...], x1l[...]))
    l1 = jnp.where(gone0 | gone1, 0.0, l1)
    l1s = split(l1)
    lh = jnp.concatenate([l0s[0], l1s[0]], axis=1)
    ll = jnp.concatenate([l0s[1], l1s[1]], axis=1)
    for j in range(cols // W):
        sl = slice(j * W, (j + 1) * W)
        f = masked(front[:, sl], 2, 2, aq * 2, j * 2, fill, shift, g == b)
        f = f - mm3((lh, ll), (uh[:, sl], ul[:, sl]))
        f = jnp.where((g == r0) & (q0 == j) & jnp.logical_not(gone0), l0, f)
        if j == 3:
            f = jnp.where(g == LAST, jnp.where(gone0 | gone1, c1, l1), f)
        out[:, sl] = f
    here = pl.ds(pl.multiple_of(aq * W, W), W)
    h = jnp.concatenate([hbuf[:, 0, here], hbuf[:, 1, here]], axis=0)
    h = h - mm3t((pvh[...], pvl[...]), (lh, ll))
    hout[0, :, here] = h[0:16]
    hout[1, :, here] = h[16:32]


def per_device(front, diag, fill, supernodes, loads):
    rows, cols = front.shape
    order = rows * lax.axis_size("blk")
    g, b = lax.axis_index("grp"), lax.axis_index("blk")
    sc = jnp.stack([supernodes[0], supernodes[1], g, b]).astype(jnp.int32)
    shift = (diag * math.sqrt(order)).reshape(rows // BS, BS)
    smem = pl.BlockSpec(memory_space=pltpu.SMEM)

    def const(shape):
        return pl.BlockSpec(shape, lambda u, sc: (0,) * len(shape))

    cbuf, rbuf, piv = pl.pallas_call(
        prep_kernel,
        out_shape=(
            jax.ShapeDtypeStruct((2, 4, 256, W), F32),
            jax.ShapeDtypeStruct((2, W, cols), F32),
            jax.ShapeDtypeStruct((2, 2 * W), F32),
        ),
        grid_spec=pltpu.PrefetchScalarGridSpec(
            num_scalar_prefetch=1,
            grid=(4,),
            in_specs=[
                smem,
                pl.BlockSpec((W, cols), lambda u, sc: (quarter_of(u, sc[0], sc[3]), 0)),
                pl.BlockSpec((W, W), lambda u, sc: ((sc[0] % 8) // 2, u)),
                pl.BlockSpec((W, W), lambda u, sc: (3, u)),
                const(shift.shape),
                const(loads.shape),
            ],
            out_specs=(
                pl.BlockSpec((2, 4, 64, W), lambda u, sc: (0, 0, u, 0)),
                pl.BlockSpec((2, W, W), lambda u, sc: (0, 0, u)),
                const((2, 2 * W)),
            ),
        ),
        name="panels",
    )(sc, fill, front, front, front, shift, loads)
    rbuf = rbuf.reshape(2, 2, 4, 32, cols)
    cbuf, rbuf, dbuf, hbuf, pbuf = lax.switch(
        supernodes[0] // 8, [functools.partial(comm, r) for r in range(16)], cbuf, rbuf, loads, piv)
    rbuf = rbuf.reshape(2, W, cols)
    out, hout = pl.pallas_call(
        update_kernel,
        out_shape=(
            jax.ShapeDtypeStruct((rows, cols), F32),
            jax.ShapeDtypeStruct((2, 16, rows), F32),
        ),
        grid_spec=pltpu.PrefetchScalarGridSpec(
            num_scalar_prefetch=1,
            grid=(4,),
            in_specs=[
                smem,
                pl.BlockSpec((W, cols), lambda u, sc: (quarter_of(u, sc[0], sc[3]), 0)),
                const(shift.shape),
                pl.BlockSpec((2, 4, 64, W), lambda u, sc: (0, 0, u, 0)),
                const(rbuf.shape),
                const(dbuf.shape),
                const(hbuf.shape),
                const(pbuf.shape),
            ],
            out_specs=(
                pl.BlockSpec((W, cols), lambda u, sc: (quarter_of(u, sc[0], sc[3]), 0)),
                const((2, 16, rows)),
            ),
            scratch_shapes=[pltpu.VMEM((W, W), BF16)] * 6
            + [pltpu.VMEM((2 * W, cols), BF16)] * 2
            + [pltpu.VMEM((32, 2 * W), BF16)] * 2,
        ),
        name="update",
    )(sc, fill, front, shift, cbuf, rbuf, dbuf, hbuf, pbuf)
    return out, jnp.swapaxes(hout, 0, 1).reshape(32, rows)


def solution(mesh):
    in_specs = (P("blk", "grp"), P("blk"), P("blk", "grp"), P(), P(("grp", "blk"), None))
    out_specs = (P("blk", "grp"), P("grp", "blk"))
    return jax.shard_map(
        per_device, mesh=mesh, in_specs=in_specs, out_specs=out_specs, check_vma=False
    )
```

time: 788 us -> 124 us (0.16)
  the two profiles are of different devices: /device:TPU:1 before, /device:TPU:5 now
where the time goes in v1:
time: 124 us; the launch traced here: 123 us
  Pallas kernels  107 us (86%)
  loops' own time  9.25 us (7%)
  between operations  3.25 us (3%)
  other arithmetic  2.6 us (2%)
  local copies, waits for them, and re-layouts  1.76 us (1%)
    pallas_call x1, Pallas kernels, comm(): pl.pallas_call(functools.partial(comm_kernel, r0), out_shape=(jax.ShapeDt...  83.2 us
    pallas_call x1, Pallas kernels, per_device(): pl.pallas_call(update_kernel, out_shape=(jax.ShapeDtypeStruct((rows, cols...  17.5 us
    another operation x1, loops' own time, per_device(): lax.switch(supernodes[0] // 8, [functools.partial(comm, r) for r in range...  9.25 us
    pallas_call x1, Pallas kernels, per_device(): pl.pallas_call(prep_kernel, out_shape=(jax.ShapeDtypeStruct((2, 4, 256, W...  5.94 us

profile of v1, /device:TPU:5, one launch (start us, length us, event | category | flops | bytes accessed | tf_op | source)
XLA Modules:
  0.0 123.5 jit_solution(7312233632588736500)
XLA Ops:
  3.2 1.3 %pad_add_fusion.sc = s32[4]{0:T(128)} fusion(s32[1]{0:T(128)} %bitcast.17, s32[1]{0:T(128)} %bitcast.16, s32[2]{0:T(128)} %param.24), kind=kLoop, calls=%fused_computation.1 | loop fusion | flops 8 | bytes 32 | tf_op jit(solution)/shard_map/stack | solution.py:410
  4.6 1.3 %multiply_bitcast_fusion.shift = f32[8,128]{1,0:T(8,128)} fusion(f32[1024]{0:T(1024)} %param.22), kind=kLoop, calls=%fused_computation | loop fusion | flops 1024 | bytes 8192 | tf_op jit(solution)/shard_map/reshape | solution.py:411
  5.8 0.0 copy-start
  5.8 5.9 %panels.1 = (f32[2,4,256,256]{3,2,1,0:T(8,128)S(1)}, f32[2,256,1024]{2,1,0:T(8,128)}, f32[2,512]{1,0:T(2,128)S(1)}) custom-call(s32[4]{0:T(128)} %pad_add_fusion.sc, s32[8,8]{1,0:T(8,128)} %fill.3, f32[1024,1024]{1,0:T(8,128)} %front.3, f32[1024,1024]{1,0:T(8,128)} %front.3, f32[1024,1024]{1,0:T(8,128)} %front.3, f32[8,128]{1,0:T(8,128)} %multiply_bitcast_fusion.shift, ...), custom_call_target="tpu_custom_call" | custom-call | tf_op jit(solution)/shard_map/panels/pallas_call | solution.py:417
  11.8 0.0 copy-done
  11.8 92.4 %conditional.1 = (f32[2,4,256,256]{3,2,1,0:T(8,128)S(1)}, f32[2,2,4,64,256]{4,3,2,1,0:T(8,128)S(1)}, f32[16,2,1024]{2,1,0:T(2,128)S(1)}, f32[16,2,512]{2,1,0:T(2,128)S(1)}, f32[2,256,1024]{2,1,0:T(8,128)}) conditional(s32[]{:T(128)} %clamp.3, (f32[2,4,256,256]{3,2,1,0:T(8,128)S(1)}, f32[2,2,4,32,1024]{4,3,2,1,0:T(8,128)}, ...), branch_computations={%region_0.1_spmd, %region_1.2_spmd, %region_2.3_spmd, %region_3.4_... | conditional | bytes 40 | solution.py:444
  20.9 83.2 %exchange_8.1 = (f32[2,4,256,256]{3,2,1,0:T(8,128)S(1)}, f32[2,2,4,32,1024]{4,3,2,1,0:T(8,128)}, f32[2,2,4,64,256]{4,3,2,1,0:T(8,128)S(1)}, f32[16,2,1024]{2,1,0:T(2,128)S(1)}, f32[16,2,512]{2,1,0:T(2,128)S(1)}) custom-call(f32[2,4,256,256]{3,2,1,0:T(8,128)S(1)} %get-tuple-element.281.cin, ...), custom_call_target="tpu_custom_call", output_to_operand_aliasing={{0}: (0, {}), {1}: (1, {})} | custom-call | tf_op jit(solution)/shard_map/cond/branch_8_fun/exchange_8/pallas_call | solution.py:283
  104.2 17.5 %update.1 = (f32[1024,1024]{1,0:T(8,128)}, f32[2,16,1024]{2,1,0:T(8,128)}) custom-call(s32[4]{0:T(128)} %pad_add_fusion.sc, s32[8,8]{1,0:T(8,128)} %fill.3, f32[1024,1024]{1,0:T(8,128)} %front.3, f32[8,128]{1,0:T(8,128)} %multiply_bitcast_fusion.shift, f32[2,4,256,256]{3,2,1,0:T(8,128)S(1)} %get-tuple-element.368.cbuf, ...), custom_call_target="tpu_custom_call" | custom-call | tf_op jit(solution)/shard_map/update/pallas_call | solution.py:447
  121.7 1.0 copy.39
  122.7 0.7 reshape.48
Async XLA Ops:
  5.8 5.9 %copy-start = (f32[2,16384]{1,0:T(2,128)S(1)}, f32[2,16384]{1,0:T(2,128)}, u32[]{:S(2)}) copy-start(f32[2,16384]{1,0:T(2,128)} %loads.1) | copy-start | bytes 393220

commit v2 on v1

v2 whole, which is shorter than its diff:
```python
import functools
import math

import jax
import jax.numpy as jnp
from jax import lax
from jax.experimental import pallas as pl
from jax.experimental.pallas import tpu as pltpu
from jax.sharding import PartitionSpec as P

MESH = pl.DeviceIdType.MESH
HIGH = lax.Precision.HIGHEST
F32 = jnp.float32
BF16 = jnp.bfloat16

BS = 128
W = 256
NS_STEPS = 3
CH = 32
N = 256 // CH
LG = 1
NR = 4
LAST = 15


def quarter_of(u, s0, b):
    r0, q0 = s0 // 8, (s0 % 8) // 2
    first = jnp.where(b == r0, q0, jnp.where(b == LAST, 3, 0))
    both = (b == r0) & (b == LAST)

    def swap(v):
        return jnp.where(v == 0, first, jnp.where(v == first, 0, v))

    v = jnp.where(both & (u == 1), 3, jnp.where(both & (u == 3), 1, u))
    return swap(v)


def masked(weight, values, rows, cols, row0, col0, fill_ref, shift, on_diag):
    out = []
    for i in range(rows):
        line = []
        for j in range(cols):
            v = values[i * BS : (i + 1) * BS, j * BS : (j + 1) * BS]
            v = jnp.where(fill_ref[row0 + i, col0 + j] > 0, v, 0.0)
            same = on_diag & (row0 + i == col0 + j)
            r = lax.broadcasted_iota(jnp.int32, (BS, BS), 0)
            c = lax.broadcasted_iota(jnp.int32, (BS, BS), 1)
            d = shift[pl.ds(row0 + i, 1), :] * weight
            v = v + jnp.where((r == c) & same, d, 0.0)
            line.append(v)
        out.append(jnp.concatenate(line, axis=1) if cols > 1 else line[0])
    return jnp.concatenate(out, axis=0) if rows > 1 else out[0]


def prep_kernel(weight, sc, fill, front, top0, top1, shift, loads, cbuf, rbuf, piv):
    u = pl.program_id(0)
    s0, g, b = sc[0], lax.axis_index("grp"), lax.axis_index("blk")
    q0 = (s0 % 8) // 2
    aq = quarter_of(u, s0, b)
    diag = g == b
    for k, q in ((0, q0), (1, 3)):
        v = front[:, pl.ds(pl.multiple_of(q * W, W), W)]
        v = masked(weight, v, 2, 2, aq * 2, q * 2, fill, shift, diag)
        cbuf[k] = v.reshape(4, 64, W)
        t = (top0, top1)[k][...]
        rbuf[k] = masked(weight, t, 2, 2, q * 2, u * 2, fill, shift, diag)
    piv[:, 0:W] = loads[:, pl.ds(pl.multiple_of(s0 * BS, W), W)]
    piv[:, W : 2 * W] = loads[:, loads.shape[1] - W :]


def comm_kernel(r0, cin, rin, loads, piv, cbuf, rbuf, dbuf, hbuf, pbuf,
                cs, cz, cr, rs, rx, rown, roth, ds, dx, down, doth, hs, hr, loc):
    g, b = lax.axis_index("grp"), lax.axis_index("blk")
    y, zl = g // 4, g % 4
    x, zh, c = b // 4, (b // 2) % 2, b % 2
    partner = {"blk": x * 4 + zh * 2 + (1 - c)}
    cross = {"blk": x * 4 + (1 - zh) * 2 + c}

    def xto(i):
        return {"blk": ((x + i) % 4) * 4 + zh * 2 + c}

    def yto(i):
        return {"grp": ((y + i) % 4) * 4 + zl}

    def zto(i):
        return {"grp": y * 4 + i}

    barrier = pltpu.get_barrier_semaphore()

    @pl.loop(1, 16)
    def _(i):
        pl.semaphore_signal(barrier, inc=1, device_id={"blk": (b + i) % 16}, device_id_type=MESH)

    @pl.loop(1, 4)
    def _(i):
        pl.semaphore_signal(barrier, inc=1, device_id=yto(i), device_id_type=MESH)
        pl.semaphore_signal(barrier, inc=1, device_id=zto((zl + i) % 4), device_id_type=MESH)

    pl.semaphore_wait(barrier, 21)

    def rdma(src, dst, ssem, rsem, to):
        return pltpu.make_async_remote_copy(
            src_ref=src, dst_ref=dst, send_sem=ssem, recv_sem=rsem, device_id=to, device_id_type=MESH)

    nots = jnp.logical_not
    place = (0, 1 if r0 == LAST else 0)

    def pick(k, first, second):
        return jnp.where(k == 0, first, second)

    def way(cls):
        return jnp.where(cls < 2, 1, 3), jnp.where(cls < 2, 3, 1)

    def ring(pos, root):
        a = (pos + 4 - root) % 4
        own = jnp.where(a == 3, 2, jnp.where(a == 2, 3, a))
        return a, own, jnp.where(a == 3, 1, a)

    def cplan(k):
        yk, zk = pick(k, r0 // 4, LAST // 4), pick(k, r0 % 4, LAST % 4)
        a, own, hop = ring(y, yk)
        e = jnp.where(zl > zk, zl - zk, zk - zl)
        lag = (hop + jnp.where(e == 0, 0, jnp.where(e == 3, 2, 1))) * LG
        return a, own, e == 0, lag, zk

    def rplan(k):
        xk, hk, ck = pick(k, r0 // 4, 3), pick(k, (r0 // 2) % 2, 1), pick(k, r0 % 2, 1)
        a, own, hop = ring(x, xk)
        inside = zh == hk
        lag = (hop + jnp.where(inside, 0, 2) + jnp.where(c == ck, 0, 1)) * LG
        return a, own, inside, lag, inside & (a == 0) & (c == ck), inside & (a == 0) & (c != ck)

    def waits(a, own, inside, origin, cls):
        return jnp.where(inside, nots(origin) & (a == way(cls)[1]), cls != own)

    def crow(k, cls, n):
        return cbuf.at[k, cls, pl.ds(pl.multiple_of(n * CH, CH), CH), :]

    def csend(k, cls, n, sem, to):
        rdma(crow(k, cls, n), crow(k, cls, n), sem, cr.at[k, cls, n], to).start()

    def cwait(k, cls, n):
        rdma(crow(k, cls, n), crow(k, cls, n), cs.at[k, 0], cr.at[k, cls, n], yto(1)).wait_recv()

    def rrow(k, half, cls, n):
        return rbuf.at[k, half, cls, pl.ds(pl.multiple_of(n * 8, 8), 8), :]

    def rsend(k, half, cls, n, sem, to):
        rdma(rrow(k, half, cls, n), rrow(k, half, cls, n), sem, rown.at[k, cls, n], to).start()

    def rwait(k, cls, n):
        rdma(rrow(k, c, cls, n), rrow(k, c, cls, n), rs.at[k, 0], rown.at[k, cls, n], xto(1)).wait_recv()

    def drow(k, cls, half):
        return dbuf.at[k, :, cls, pl.ds(pl.multiple_of(half * 32, 32), 32), :]

    def dsource(k, cls, half):
        at = pl.multiple_of(pick(k, place[0], place[1]) * 64 + half * 32, 32)
        return cbuf.at[:, cls, pl.ds(at, 32), :]

    def dsend(k, cls, sem, to):
        rdma(drow(k, cls, c), drow(k, cls, c), sem, down.at[k, cls], to).start()

    def dwait(k, cls):
        rdma(drow(k, cls, c), drow(k, cls, c), ds.at[k, 0], down.at[k, cls], xto(1)).wait_recv()

    early = [(p + 1) * (64 // CH) for p in place]
    tds = [4 * LG + e - 1 for e in early]
    turns = max(N + 4 * LG, max(tds) + 1 + 5 * LG)

    def cfinal(lo, hi):
        @pl.loop(0, 2)
        def _(k):
            a, own, inside, lag, zk = cplan(k)

            @pl.loop(0, 4)
            def _(cls):
                @pl.when(waits(a, own, inside, a == 0, cls))
                def _():
                    @pl.loop(lo, hi)
                    def _(n):
                        cwait(k, cls, n)

    def mine(k):
        return pltpu.make_async_copy(cbuf.at[:, :, pl.ds(place[k] * 64, 64), :], dbuf.at[k], loc.at[2 + k])

    own_h = [
        pltpu.make_async_copy(loads.at[:, pl.ds(pl.multiple_of(b * 1024, 1024), 1024)], hbuf.at[b], loc.at[0]),
        pltpu.make_async_copy(piv, pbuf.at[b], loc.at[1]),
    ]

    @pl.loop(0, turns)
    def _(t):
        @pl.loop(0, 2)
        def _(k):
            a, own, inside, lag, zk = cplan(k)
            n = t - lag
            on = (n >= 0) & (n < N)

            @pl.when(on & inside)
            def _():
                @pl.loop(0, 4)
                def _(cls):
                    step, end = way(cls)

                    @pl.when(a != end)
                    def _():
                        @pl.when(a != 0)
                        def _():
                            cwait(k, cls, n)

                        csend(k, cls, n, cs.at[k, cls], yto(step))

                @pl.loop(0, 4)
                def _(z):
                    @pl.when((z != zl) & (z - zl < 3) & (zl - z < 3))
                    def _():
                        csend(k, own, n, cz.at[k, z], zto(z))

            @pl.when(on & nots(inside))
            def _():
                cwait(k, own, n)

                @pl.when(((zk == 0) & (zl == 2)) | ((zk == 3) & (zl == 1)))
                def _():
                    csend(k, own, n, cz.at[k, 0], zto(3 - zk))

                @pl.loop(1, 4)
                def _(i):
                    j = jnp.where(i == 1, 2, jnp.where(i == 2, 1, 3))
                    csend(k, own, n, cs.at[k, j], yto(j))

            a, own, inside, lag, root, mate = rplan(k)
            n = t - lag
            on = (n >= 0) & (n < NR)

            @pl.when(on & inside)
            def _():
                @pl.loop(0, 4)
                def _(cls):
                    step, end = way(cls)

                    @pl.when(root)
                    def _():
                        rsend(k, 1 - c, cls, n, rx.at[k, 1], partner)

                    @pl.when(a != end)
                    def _():
                        @pl.when(nots(root))
                        def _():
                            rwait(k, cls, n)

                        rsend(k, c, cls, n, rs.at[k, cls], xto(step))

                rsend(k, c, own, n, rx.at[k, 0], cross)

            @pl.when(on & nots(inside))
            def _():
                rwait(k, own, n)

                @pl.loop(1, 4)
                def _(i):
                    j = jnp.where(i == 1, 2, jnp.where(i == 2, 1, 3))
                    rsend(k, c, own, n, rs.at[k, j], xto(j))

        @pl.when(t == 2)
        def _():
            for m in own_h:
                m.start()

            @pl.loop(1, 16)
            def _(i):
                to = (b + i) % 16
                cols = pl.ds(pl.multiple_of(to * 1024, 1024), 1024)
                rdma(loads.at[:, cols], hbuf.at[b], hs.at[0], hr.at[0, i], {"blk": to}).start()
                rdma(piv, pbuf.at[b], hs.at[1], hr.at[1, i], {"blk": to}).start()

        for i, td in enumerate(sorted(set(tds))):
            @pl.when(t == td)
            def _():
                cfinal(0 if i == 0 else early[0], td - 4 * LG + 1)
                for k in range(2):
                    if tds[k] == td:
                        @pl.when(b == (r0, LAST)[k])
                        def _():
                            mine(k).start()

        @pl.loop(0, 2)
        def _(k):
            a, own, inside, lag, root, mate = rplan(k)
            on = t - lag == pick(k, tds[0], tds[1])

            @pl.when(on & inside)
            def _():
                @pl.loop(0, 4)
                def _(cls):
                    step, end = way(cls)

                    @pl.when(root)
                    def _():
                        rdma(dsource(k, cls, 1 - c), drow(k, cls, 1 - c), dx.at[k, 1], down.at[k, cls],
                             partner).start()
                        rdma(dsource(k, cls, c), drow(k, cls, c), ds.at[k, cls], down.at[k, cls],
                             xto(step)).start()

                    @pl.when(nots(root) & (a != end))
                    def _():
                        dwait(k, cls)
                        dsend(k, cls, ds.at[k, cls], xto(step))

                @pl.when(root)
                def _():
                    rdma(dsource(k, 0, c), drow(k, 0, c), dx.at[k, 0], down.at[k, 0], cross).start()

                    @pl.loop(0, 4)
                    def _(cls):
                        rdma(dsource(k, cls, c), drow(k, cls, c), dx.at[k, 2], doth.at[k, cls], partner).start()

                @pl.when(nots(root))
                def _():
                    dsend(k, own, dx.at[k, 0], cross)

            @pl.when(on & nots(inside))
            def _():
                dwait(k, own)

                @pl.loop(1, 4)
                def _(i):
                    j = jnp.where(i == 1, 2, jnp.where(i == 2, 1, 3))
                    dsend(k, own, ds.at[k, j], xto(j))

    @pl.loop(0, 2)
    def _(k):
        a, own, inside, lag, root, mate = rplan(k)

        @pl.loop(0, 4)
        def _(cls):
            @pl.when(waits(a, own, inside, a == 0, cls))
            def _():
                @pl.loop(0, NR)
                def _(n):
                    rwait(k, cls, n)

            @pl.when(nots(mate))
            def _():
                half = rbuf.at[k, c, cls]
                rdma(half, half, rx.at[k, 2], roth.at[k, cls], partner).start()

    @pl.loop(0, 2)
    def _(k):
        a, own, inside, lag, root, mate = rplan(k)

        @pl.loop(0, 4)
        def _(cls):
            @pl.when(waits(a, own, inside, a == 0, cls))
            def _():
                dwait(k, cls)

            @pl.when(nots(mate | root))
            def _():
                rdma(drow(k, cls, c), drow(k, cls, c), dx.at[k, 2], doth.at[k, cls], partner).start()

    cfinal(max(early), N)

    @pl.loop(1, 16)
    def _(i):
        rdma(piv, pbuf.at[b], hs.at[1], hr.at[1, i], partner).wait_recv()
        rdma(hbuf.at[b], hbuf.at[b], hs.at[0], hr.at[0, i], partner).wait_recv()

    @pl.loop(0, 2)
    def _(k):
        a, own, inside, lag, root, mate = rplan(k)

        @pl.when(nots(root))
        def _():
            @pl.loop(0, 4)
            def _(cls):
                rest = rbuf.at[k, 1 - c, cls]
                rdma(rest, rest, rx.at[k, 2], roth.at[k, cls], partner).wait_recv()
                part = drow(k, cls, 1 - c)
                rdma(part, part, dx.at[k, 2], doth.at[k, cls], partner).wait_recv()

    @pl.loop(0, 2)
    def _(k):
        ca, cown, cin_, clag, zk = cplan(k)
        a, own, inside, lag, root, mate = rplan(k)

        def csent(sem):
            rdma(cbuf.at[k, 0], cbuf.at[k, 0], sem, cr.at[k, 0, 0], yto(1)).wait_send()

        def rsent(sem):
            rdma(rbuf.at[k, c, 0], rbuf.at[k, c, 0], sem, rown.at[k, 0, 0], xto(1)).wait_send()

        def dsent(sem):
            rdma(drow(k, 0, c), drow(k, 0, c), sem, down.at[k, 0], xto(1)).wait_send()

        @pl.loop(0, 4)
        def _(i):
            @pl.when(jnp.where(cin_, ca != way(i)[1], i > 0))
            def _():
                csent(cs.at[k, i])

            @pl.when(jnp.where(inside, a != way(i)[1], i > 0))
            def _():
                rsent(rs.at[k, i])
                dsent(ds.at[k, i])

            far = (i == 0) & (((zk == 0) & (zl == 2)) | ((zk == 3) & (zl == 1)))

            @pl.when(jnp.where(cin_, (i != zl) & (i - zl < 3) & (zl - i < 3), far))
            def _():
                csent(cz.at[k, i])

        @pl.when(inside)
        def _():
            rsent(rx.at[k, 0])
            dsent(dx.at[k, 0])

        def whole(sem, dsem):
            rdma(rbuf.at[k, 0], rbuf.at[k, 0], sem, rown.at[k, 0, 0], xto(1)).wait_send()
            part = dbuf.at[k, :, :, 0:32, :]
            rdma(part, part, dsem, down.at[k, 0], xto(1)).wait_send()

        @pl.when(root)
        def _():
            whole(rx.at[k, 1], dx.at[k, 1])

        @pl.when(nots(mate))
        def _():
            whole(rx.at[k, 2], dx.at[k, 2])

    for k in range(2):
        @pl.when(b == (r0, LAST)[k])
        def _():
            mine(k).wait()
    for m in own_h:
        m.wait()

    @pl.loop(1, 16)
    def _(i):
        rdma(hbuf.at[b], hbuf.at[b], hs.at[0], hr.at[0, i], partner).wait_send()
        rdma(piv, pbuf.at[b], hs.at[1], hr.at[1, i], partner).wait_send()


def comm(r0, cbuf, rbuf, loads, piv):
    anyspec = pl.BlockSpec(memory_space=pl.ANY)
    dma = pltpu.SemaphoreType.DMA
    return pl.pallas_call(
        functools.partial(comm_kernel, r0),
        out_shape=(
            jax.ShapeDtypeStruct(cbuf.shape, F32),
            jax.ShapeDtypeStruct(rbuf.shape, F32),
            jax.ShapeDtypeStruct((2, 2, 4, 64, W), F32),
            jax.ShapeDtypeStruct((16, 2, 1024), F32),
            jax.ShapeDtypeStruct((16, 2, 2 * W), F32),
        ),
        in_specs=[anyspec] * 4,
        out_specs=(anyspec,) * 5,
        input_output_aliases={0: 0, 1: 1},
        scratch_shapes=[
            dma((2, 4)), dma((2, 4)), dma((2, 4, N)),
            dma((2, 4)), dma((2, 3)), dma((2, 4, NR)), dma((2, 4)),
            dma((2, 4)), dma((2, 3)), dma((2, 4)), dma((2, 4)),
            dma((2,)), dma((2, 16)), dma((4,)),
        ],
        compiler_params=pltpu.CompilerParams(collective_id=r0, has_side_effects=True),
        name="exchange_%d" % r0,
    )(cbuf, rbuf, loads, piv)


def split(v):
    hi = v.astype(BF16)
    return hi, (v - hi.astype(F32)).astype(BF16)


def mm(a, b):
    return jnp.dot(a, b, preferred_element_type=F32)


def mm3(a, b):
    return mm(a[0], b[0]) + (mm(a[0], b[1]) + mm(a[1], b[0]))


def mm3t(a, b):
    dims = (((1,), (1,)), ((), ()))

    def one(p, q):
        return lax.dot_general(p, q, dims, preferred_element_type=F32)

    return one(a[0], b[0]) + (one(a[0], b[1]) + one(a[1], b[0]))


def full(a, b):
    return jnp.dot(a, b, precision=HIGH, preferred_element_type=F32)


def newton(pivot):
    n = pivot.shape[0]
    r = lax.broadcasted_iota(jnp.int32, (n, n), 0)
    c = lax.broadcasted_iota(jnp.int32, (n, n), 1)
    eye = r == c
    kept = jnp.where(eye, pivot, 0.0)
    drow = 1.0 / jnp.sum(kept, axis=0, keepdims=True)
    dcol = 1.0 / jnp.sum(kept, axis=1, keepdims=True)
    inv = jnp.where(eye, 2.0 * drow, 0.0) - dcol * (pivot * drow)
    for _ in range(NS_STEPS - 1):
        inv = 2.0 * inv - full(inv, full(pivot, inv))
    return inv


def update_kernel(weight, sc, fill, front, shift, cbuf, rbuf, dbuf, hbuf, pbuf, out, hout,
                  x0h, x0l, x1h, x1l, d1h, d1l, uh, ul, pvh, pvl, hs, weave):
    u = pl.program_id(0)
    s0, g, b = sc[0], lax.axis_index("grp"), lax.axis_index("blk")
    r0, q0 = s0 // 8, (s0 % 8) // 2
    cols = front.shape[1]
    ids = lax.broadcasted_iota(jnp.int32, (1, cols), 1) // W
    dead0 = (g == r0) & (ids == q0)
    dead1 = (g == LAST) & (ids == 3)

    @pl.when(u == 0)
    def _():
        d = [[dbuf[i, j].reshape(W, W) for j in range(2)] for i in range(2)]
        x0 = newton(d[0][0])
        m = full(d[1][0], x0)
        x1 = newton(d[1][1] - full(m, d[0][1]))
        x0h[...], x0l[...] = split(x0)
        x1h[...], x1l[...] = split(x1)
        d1h[...], d1l[...] = split(d[0][1])
        ms = split(m)
        u0 = jnp.where(dead0, 0.0, rbuf[0])
        u0s = split(u0)
        u1 = jnp.where(dead0 | dead1, 0.0, rbuf[1] - mm3(ms, u0s))
        u1s = split(u1)
        uh[0:W], ul[0:W] = u0s
        uh[W : 2 * W], ul[W : 2 * W] = u1s
        pv = jnp.concatenate([pbuf[:, 0, :], pbuf[:, 1, :]], axis=0)
        p0 = split(pv[:, 0:W])
        p1 = split(pv[:, W : 2 * W] - mm3t(p0, ms))
        pvh[:, 0:W], pvl[:, 0:W] = p0
        pvh[:, W : 2 * W], pvl[:, W : 2 * W] = p1

    aq = quarter_of(u, s0, b)
    gone0 = (b == r0) & (aq == q0)
    gone1 = (b == LAST) & (aq == 3)
    c0 = cbuf[0].reshape(W, W)
    l0 = mm3(split(c0), (x0h[...], x0l[...]))
    l0 = jnp.where(gone0, 0.0, l0)
    l0s = split(l0)
    c1 = cbuf[1].reshape(W, W) - mm3(l0s, (d1h[...], d1l[...]))
    l1 = mm3(split(c1), (x1h[...], x1l[...]))
    l1 = jnp.where(gone0 | gone1, 0.0, l1)
    l1s = split(l1)
    lh = jnp.concatenate([l0s[0], l1s[0]], axis=1)
    ll = jnp.concatenate([l0s[1], l1s[1]], axis=1)
    for j in range(cols // W):
        sl = slice(j * W, (j + 1) * W)
        f = masked(weight, front[:, sl], 2, 2, aq * 2, j * 2, fill, shift, g == b)
        f = f - mm3((lh, ll), (uh[:, sl], ul[:, sl]))
        f = jnp.where((g == r0) & (q0 == j) & jnp.logical_not(gone0), l0, f)
        if j == 3:
            f = jnp.where(g == LAST, jnp.where(gone0 | gone1, c1, l1), f)
        out[:, sl] = f
    here = pl.ds(pl.multiple_of(aq * W, W), W)
    h = jnp.concatenate([hbuf[:, 0, here], hbuf[:, 1, here]], axis=0)
    h = h - mm3t((pvh[...], pvl[...]), (lh, ll))
    hs[:, here] = h

    @pl.when(u == 3)
    def _():
        for j in range(cols // BS):
            lanes = slice(j * BS, (j + 1) * BS)
            weave[j, pl.ds(0, 16, stride=2), :] = hs[0:16, lanes]
            weave[j, pl.ds(1, 16, stride=2), :] = hs[16:32, lanes]
            hout[:, lanes] = weave[j]


def per_device(front, diag, fill, supernodes, loads):
    rows, cols = front.shape
    order = rows * lax.axis_size("blk")
    sc = supernodes
    weight = math.sqrt(order)
    shift = diag.reshape(rows // BS, BS)
    smem = pl.BlockSpec(memory_space=pltpu.SMEM)

    def const(shape):
        return pl.BlockSpec(shape, lambda u, sc: (0,) * len(shape))

    cbuf, rbuf, piv = pl.pallas_call(
        functools.partial(prep_kernel, weight),
        out_shape=(
            jax.ShapeDtypeStruct((2, 4, 256, W), F32),
            jax.ShapeDtypeStruct((2, W, cols), F32),
            jax.ShapeDtypeStruct((2, 2 * W), F32),
        ),
        grid_spec=pltpu.PrefetchScalarGridSpec(
            num_scalar_prefetch=1,
            grid=(4,),
            in_specs=[
                smem,
                pl.BlockSpec((W, cols), lambda u, sc: (quarter_of(u, sc[0], lax.axis_index("blk")), 0)),
                pl.BlockSpec((W, W), lambda u, sc: ((sc[0] % 8) // 2, u)),
                pl.BlockSpec((W, W), lambda u, sc: (3, u)),
                const(shift.shape),
                const(loads.shape),
            ],
            out_specs=(
                pl.BlockSpec((2, 4, 64, W), lambda u, sc: (0, 0, u, 0)),
                pl.BlockSpec((2, W, W), lambda u, sc: (0, 0, u)),
                const((2, 2 * W)),
            ),
        ),
        name="panels",
    )(sc, fill, front, front, front, shift, loads)
    rbuf = rbuf.reshape(2, 2, 4, 32, cols)
    cbuf, rbuf, dbuf, hbuf, pbuf = lax.switch(
        supernodes[0] // 8, [functools.partial(comm, r) for r in range(16)], cbuf, rbuf, loads, piv)
    rbuf = rbuf.reshape(2, W, cols)
    out, hout = pl.pallas_call(
        functools.partial(update_kernel, weight),
        out_shape=(
            jax.ShapeDtypeStruct((rows, cols), F32),
            jax.ShapeDtypeStruct((32, rows), F32),
        ),
        grid_spec=pltpu.PrefetchScalarGridSpec(
            num_scalar_prefetch=1,
            grid=(4,),
            in_specs=[
                smem,
                pl.BlockSpec((W, cols), lambda u, sc: (quarter_of(u, sc[0], lax.axis_index("blk")), 0)),
                const(shift.shape),
                pl.BlockSpec((2, 4, 64, W), lambda u, sc: (0, 0, u, 0)),
                const(rbuf.shape),
                const(dbuf.shape),
                const(hbuf.shape),
                const(pbuf.shape),
            ],
            out_specs=(
                pl.BlockSpec((W, cols), lambda u, sc: (quarter_of(u, sc[0], lax.axis_index("blk")), 0)),
                const((32, rows)),
            ),
            scratch_shapes=[pltpu.VMEM((W, W), BF16)] * 6
            + [pltpu.VMEM((2 * W, cols), BF16)] * 2
            + [pltpu.VMEM((32, 2 * W), BF16)] * 2
            + [pltpu.VMEM((32, rows), F32), pltpu.VMEM((rows // BS, 32, BS), F32)],
        ),
        name="update",
    )(sc, fill, front, shift, cbuf, rbuf, dbuf, hbuf, pbuf)
    return out, hout


def solution(mesh):
    in_specs = (P("blk", "grp"), P("blk"), P("blk", "grp"), P(), P(("grp", "blk"), None))
    out_specs = (P("blk", "grp"), P("grp", "blk"))
    return jax.shard_map(
        per_device, mesh=mesh, in_specs=in_specs, out_specs=out_specs, check_vma=False
    )
```

time: 124 us -> 90.7 us (0.73)
  the two profiles are of different devices: /device:TPU:5 before, /device:TPU:1 now
where the time goes in v2:
time: 90.7 us; the launch traced here: 90.5 us
  Pallas kernels  87 us (96%)
  between operations  3.25 us (4%)
    pallas_call x1, Pallas kernels, comm(): pl.pallas_call(functools.partial(comm_kernel, r0), out_shape=(jax.ShapeDt...  63 us
    pallas_call x1, Pallas kernels, per_device(): pl.pallas_call(functools.partial(update_kernel, weight), out_shape=(jax.S...  18 us
    pallas_call x1, Pallas kernels, per_device(): pl.pallas_call(functools.partial(prep_kernel, weight), out_shape=(jax.Sha...  5.96 us

profile of v2, /device:TPU:1, one launch (start us, length us, event | category | flops | bytes accessed | tf_op | source)
XLA Modules:
  0.0 90.5 jit_solution(14197510159511218617)
XLA Ops:
  3.2 0.0 copy-start
  3.2 6.0 %panels.1 = (f32[2,4,256,256]{3,2,1,0:T(8,128)S(1)}, f32[2,256,1024]{2,1,0:T(8,128)}, f32[2,512]{1,0:T(2,128)S(1)}) custom-call(s32[2]{0:T(128)} %sc.3, s32[8,8]{1,0:T(8,128)} %fill.3, f32[1024,1024]{1,0:T(8,128)} %front.3, f32[1024,1024]{1,0:T(8,128)} %front.3, f32[1024,1024]{1,0:T(8,128)} %front.3, f32[8,128]{1,0:T(8,128)} %bitcast.52, f32[2,16384]{1,0:T(2,128)} %loads.1), custom_call_target="tpu_custom_call" | custom-call | tf_op jit(solution)/shard_map/panels/pallas_call | solution.py:589
  9.2 0.0 copy-done
  9.2 63.3 %conditional.1 = (f32[2,4,256,256]{3,2,1,0:T(8,128)S(1)}, f32[2,2,4,64,256]{4,3,2,1,0:T(8,128)S(1)}, f32[16,2,1024]{2,1,0:T(2,128)S(1)}, f32[16,2,512]{2,1,0:T(2,128)S(1)}, f32[2,256,1024]{2,1,0:T(8,128)}) conditional(s32[]{:T(128)} %clamp.3, (f32[2,4,256,256]{3,2,1,0:T(8,128)S(1)}, f32[2,2,4,32,1024]{4,3,2,1,0:T(8,128)}, ...), branch_computations={%region_0.1_spmd, %region_1.2_spmd, %region_2.3_spmd, %region_3.4_... | conditional | bytes 40 | solution.py:616
  9.2 63.0 %exchange_14.1 = (f32[2,4,256,256]{3,2,1,0:T(8,128)S(1)}, f32[2,2,4,32,1024]{4,3,2,1,0:T(8,128)}, f32[2,2,4,64,256]{4,3,2,1,0:T(8,128)S(1)}, f32[16,2,1024]{2,1,0:T(2,128)S(1)}, f32[16,2,512]{2,1,0:T(2,128)S(1)}) custom-call(f32[2,4,256,256]{3,2,1,0:T(8,128)S(1)} %get-tuple-element.335.cin, ...), custom_call_target="tpu_custom_call", output_to_operand_aliasing={{0}: (0, {}), {1}: (1, {})} | custom-call | tf_op jit(solution)/shard_map/cond/branch_14_fun/exchange_14/pallas_call | solution.py:448
  72.5 18.0 %update.1 = (f32[1024,1024]{1,0:T(8,128)}, f32[32,1024]{1,0:T(8,128)}) custom-call(s32[2]{0:T(128)} %sc.3, s32[8,8]{1,0:T(8,128)} %fill.3, f32[1024,1024]{1,0:T(8,128)} %front.3, f32[8,128]{1,0:T(8,128)} %bitcast.53, f32[2,4,256,256]{3,2,1,0:T(8,128)S(1)} %get-tuple-element.366.cbuf, f32[2,256,1024]{2,1,0:T(8,128)} %get-tuple-element.367.rbuf, ...), custom_call_target="tpu_custom_call" | custom-call | tf_op jit(solution)/shard_map/update/pallas_call | solution.py:619
Async XLA Ops:
  3.2 6.0 %copy-start = (f32[2,16384]{1,0:T(2,128)S(1)}, f32[2,16384]{1,0:T(2,128)}, u32[]{:S(2)}) copy-start(f32[2,16384]{1,0:T(2,128)} %loads.1) | copy-start | bytes 393220

commit v3 on v2

--- a/solution.py
+++ b/solution.py
@@ -52,14 +52,14 @@
     return jnp.concatenate(out, axis=0) if rows > 1 else out[0]
 
 
-def prep_kernel(weight, sc, fill, front, top0, top1, shift, loads, cbuf, rbuf, piv):
+def prep_kernel(weight, sc, fill, left0, left1, top0, top1, shift, loads, cbuf, rbuf, piv):
     u = pl.program_id(0)
     s0, g, b = sc[0], lax.axis_index("grp"), lax.axis_index("blk")
     q0 = (s0 % 8) // 2
     aq = quarter_of(u, s0, b)
     diag = g == b
     for k, q in ((0, q0), (1, 3)):
-        v = front[:, pl.ds(pl.multiple_of(q * W, W), W)]
+        v = (left0, left1)[k][...]
         v = masked(weight, v, 2, 2, aq * 2, q * 2, fill, shift, diag)
         cbuf[k] = v.reshape(4, 64, W)
         t = (top0, top1)[k][...]
@@ -120,7 +120,7 @@
         yk, zk = pick(k, r0 // 4, LAST // 4), pick(k, r0 % 4, LAST % 4)
         a, own, hop = ring(y, yk)
         e = jnp.where(zl > zk, zl - zk, zk - zl)
-        lag = (hop + jnp.where(e == 0, 0, jnp.where(e == 3, 2, 1))) * LG
+        lag = (jnp.where(a == 0, 0, 1) + jnp.where(e == 0, 0, jnp.where(e >= reach, 2, 1))) * LG
         return a, own, e == 0, lag, zk
 
     def rplan(k):
@@ -133,6 +133,17 @@
     def waits(a, own, inside, origin, cls):
         return jnp.where(inside, nots(origin) & (a == way(cls)[1]), cls != own)
 
+    reach = 4 if r0 % 4 < 2 else 3
+
+    def relay(zk):
+        return (((zk == 0) & (zl == 2)) | ((zk == 3) & (zl == 1))) & (reach == 3)
+
+    def goes(a, cls):
+        return (a != way(cls)[1]) & nots((cls == 3) & (a == 3))
+
+    def cwaits(a, own, inside, cls):
+        return jnp.where(inside, (a != 0) & nots(goes(a, cls)), cls != own)
+
     def crow(k, cls, n):
         return cbuf.at[k, cls, pl.ds(pl.multiple_of(n * CH, CH), CH), :]
 
@@ -164,9 +175,21 @@
     def dwait(k, cls):
         rdma(drow(k, cls, c), drow(k, cls, c), ds.at[k, 0], down.at[k, cls], xto(1)).wait_recv()
 
+    def passing(k, a, n, count):
+        @pl.loop(0, count)
+        def _(cls):
+            @pl.when(goes(a, cls))
+            def _():
+                @pl.when(a != 0)
+                def _():
+                    cwait(k, cls, n)
+
+                csend(k, cls, n, cs.at[k, cls], yto(way(cls)[0]))
+
     early = [(p + 1) * (64 // CH) for p in place]
-    tds = [4 * LG + e - 1 for e in early]
-    turns = max(N + 4 * LG, max(tds) + 1 + 5 * LG)
+    span = (3 if reach == 3 else 2) * LG
+    tds = [span + e - 1 for e in early]
+    turns = max(N + 3 * LG, max(tds) + 1 + 5 * LG)
 
     def cfinal(lo, hi):
         @pl.loop(0, 2)
@@ -175,7 +198,7 @@
 
             @pl.loop(0, 4)
             def _(cls):
-                @pl.when(waits(a, own, inside, a == 0, cls))
+                @pl.when(cwaits(a, own, inside, cls))
                 def _():
                     @pl.loop(lo, hi)
                     def _(n):
@@ -199,29 +222,36 @@
 
             @pl.when(on & inside)
             def _():
-                @pl.loop(0, 4)
-                def _(cls):
-                    step, end = way(cls)
-
-                    @pl.when(a != end)
+                @pl.when(a == 2)
+                def _():
+                    cwait(k, 3, n)
+                    csend(k, 3, n, cs.at[k, 3], yto(3))
+
+                @pl.when(a != 2)
+                def _():
+                    @pl.when(a == 0)
                     def _():
-                        @pl.when(a != 0)
-                        def _():
-                            cwait(k, cls, n)
-
-                        csend(k, cls, n, cs.at[k, cls], yto(step))
+                        csend(k, 3, n, cz.at[k, zl], yto(2))
+
+                    passing(k, a, n, 4)
 
                 @pl.loop(0, 4)
                 def _(z):
-                    @pl.when((z != zl) & (z - zl < 3) & (zl - z < 3))
+                    @pl.when((z != zl) & (z - zl < reach) & (zl - z < reach))
                     def _():
                         csend(k, own, n, cz.at[k, z], zto(z))
 
+            late = n - LG
+
+            @pl.when(inside & (a == 2) & (late >= 0) & (late < N))
+            def _():
+                passing(k, a, late, 3)
+
             @pl.when(on & nots(inside))
             def _():
                 cwait(k, own, n)
 
-                @pl.when(((zk == 0) & (zl == 2)) | ((zk == 3) & (zl == 1)))
+                @pl.when(relay(zk))
                 def _():
                     csend(k, own, n, cz.at[k, 0], zto(3 - zk))
 
@@ -278,7 +308,7 @@
         for i, td in enumerate(sorted(set(tds))):
             @pl.when(t == td)
             def _():
-                cfinal(0 if i == 0 else early[0], td - 4 * LG + 1)
+                cfinal(0 if i == 0 else early[0], td - span + 1)
                 for k in range(2):
                     if tds[k] == td:
                         @pl.when(b == (r0, LAST)[k])
@@ -396,7 +426,7 @@
 
         @pl.loop(0, 4)
         def _(i):
-            @pl.when(jnp.where(cin_, ca != way(i)[1], i > 0))
+            @pl.when(jnp.where(cin_, goes(ca, i), i > 0))
             def _():
                 csent(cs.at[k, i])
 
@@ -405,9 +435,9 @@
                 rsent(rs.at[k, i])
                 dsent(ds.at[k, i])
 
-            far = (i == 0) & (((zk == 0) & (zl == 2)) | ((zk == 3) & (zl == 1)))
-
-            @pl.when(jnp.where(cin_, (i != zl) & (i - zl < 3) & (zl - i < 3), far))
+            near = jnp.where(i == zl, ca == 0, (i - zl < reach) & (zl - i < reach))
+
+            @pl.when(jnp.where(cin_, near, (i == 0) & relay(zk)))
             def _():
                 csent(cz.at[k, i])
 
@@ -491,7 +521,7 @@
 
 
 def full(a, b):
-    return jnp.dot(a, b, precision=HIGH, preferred_element_type=F32)
+    return mm3(split(a), split(b))
 
 
 def newton(pivot):
@@ -509,7 +539,7 @@
 
 
 def update_kernel(weight, sc, fill, front, shift, cbuf, rbuf, dbuf, hbuf, pbuf, out, hout,
-                  x0h, x0l, x1h, x1l, d1h, d1l, uh, ul, pvh, pvl, hs, weave):
+                  x0h, x0l, t1h, t1l, later, uh, ul, pvh, pvl, hs, weave):
     u = pl.program_id(0)
     s0, g, b = sc[0], lax.axis_index("grp"), lax.axis_index("blk")
     r0, q0 = s0 // 8, (s0 % 8) // 2
@@ -523,10 +553,12 @@
         d = [[dbuf[i, j].reshape(W, W) for j in range(2)] for i in range(2)]
         x0 = newton(d[0][0])
         m = full(d[1][0], x0)
-        x1 = newton(d[1][1] - full(m, d[0][1]))
+        d11 = d[1][1] - full(m, d[0][1])
+        x1 = newton(d11)
         x0h[...], x0l[...] = split(x0)
-        x1h[...], x1l[...] = split(x1)
-        d1h[...], d1l[...] = split(d[0][1])
+        t1h[0:W], t1l[0:W] = split(-full(full(x0, d[0][1]), x1))
+        t1h[W : 2 * W], t1l[W : 2 * W] = split(x1)
+        later[...] = d11
         ms = split(m)
         u0 = jnp.where(dead0, 0.0, rbuf[0])
         u0s = split(u0)
@@ -543,14 +575,12 @@
     aq = quarter_of(u, s0, b)
     gone0 = (b == r0) & (aq == q0)
     gone1 = (b == LAST) & (aq == 3)
-    c0 = cbuf[0].reshape(W, W)
-    l0 = mm3(split(c0), (x0h[...], x0l[...]))
-    l0 = jnp.where(gone0, 0.0, l0)
-    l0s = split(l0)
-    c1 = cbuf[1].reshape(W, W) - mm3(l0s, (d1h[...], d1l[...]))
-    l1 = mm3(split(c1), (x1h[...], x1l[...]))
-    l1 = jnp.where(gone0 | gone1, 0.0, l1)
-    l1s = split(l1)
+    c1 = cbuf[1].reshape(W, W)
+    c0s, c1s = split(cbuf[0].reshape(W, W)), split(c1)
+    both = tuple(jnp.concatenate([p, q], axis=1) for p, q in zip(c0s, c1s))
+    l0 = jnp.where(gone0, 0.0, mm3(c0s, (x0h[...], x0l[...])))
+    l1 = jnp.where(gone0 | gone1, 0.0, mm3(both, (t1h[...], t1l[...])))
+    l0s, l1s = split(l0), split(l1)
     lh = jnp.concatenate([l0s[0], l1s[0]], axis=1)
     ll = jnp.concatenate([l0s[1], l1s[1]], axis=1)
     for j in range(cols // W):
@@ -559,7 +589,7 @@
         f = f - mm3((lh, ll), (uh[:, sl], ul[:, sl]))
         f = jnp.where((g == r0) & (q0 == j) & jnp.logical_not(gone0), l0, f)
         if j == 3:
-            f = jnp.where(g == LAST, jnp.where(gone0 | gone1, c1, l1), f)
+            f = jnp.where(g == LAST, jnp.where(gone0, c1, jnp.where(gone1, later[...], l1)), f)
         out[:, sl] = f
     here = pl.ds(pl.multiple_of(aq * W, W), W)
     h = jnp.concatenate([hbuf[:, 0, here], hbuf[:, 1, here]], axis=0)
@@ -598,7 +628,8 @@
             grid=(4,),
             in_specs=[
                 smem,
-                pl.BlockSpec((W, cols), lambda u, sc: (quarter_of(u, sc[0], lax.axis_index("blk")), 0)),
+                pl.BlockSpec((W, W), lambda u, sc: (quarter_of(u, sc[0], lax.axis_index("blk")), (sc[0] % 8) // 2)),
+                pl.BlockSpec((W, W), lambda u, sc: (quarter_of(u, sc[0], lax.axis_index("blk")), 3)),
                 pl.BlockSpec((W, W), lambda u, sc: ((sc[0] % 8) // 2, u)),
                 pl.BlockSpec((W, W), lambda u, sc: (3, u)),
                 const(shift.shape),
@@ -611,7 +642,7 @@
             ),
         ),
         name="panels",
-    )(sc, fill, front, front, front, shift, loads)
+    )(sc, fill, front, front, front, front, shift, loads)
     rbuf = rbuf.reshape(2, 2, 4, 32, cols)
     cbuf, rbuf, dbuf, hbuf, pbuf = lax.switch(
         supernodes[0] // 8, [functools.partial(comm, r) for r in range(16)], cbuf, rbuf, loads, piv)
@@ -639,7 +670,9 @@
                 pl.BlockSpec((W, cols), lambda u, sc: (quarter_of(u, sc[0], lax.axis_index("blk")), 0)),
                 const((32, rows)),
             ),
-            scratch_shapes=[pltpu.VMEM((W, W), BF16)] * 6
+            scratch_shapes=[pltpu.VMEM((W, W), BF16)] * 2
+            + [pltpu.VMEM((2 * W, W), BF16)] * 2
+            + [pltpu.VMEM((W, W), F32)]
             + [pltpu.VMEM((2 * W, cols), BF16)] * 2
             + [pltpu.VMEM((32, 2 * W), BF16)] * 2
             + [pltpu.VMEM((32, rows), F32), pltpu.VMEM((rows // BS, 32, BS), F32)],

time: 90.7 us -> 91 us (level)
    pallas_call x1, Pallas kernels: 63 us -> 65.9 us  [comm(): pl.pallas_call(functools.partial(comm_kernel, r0), out_shape=(jax.ShapeDt...]
    pallas_call x1, Pallas kernels: 18 us -> 15.5 us  [per_device(): pl.pallas_call(functools.partial(update_kernel, weight), out_shape=(jax.S...]
where the time goes in v3:
time: 91 us; the launch traced here: 90.5 us
  Pallas kernels  86.9 us (95%)
  between operations  3.25 us (4%)
    pallas_call x1, Pallas kernels, comm(): pl.pallas_call(functools.partial(comm_kernel, r0), out_shape=(jax.ShapeDt...  65.9 us
    pallas_call x1, Pallas kernels, per_device(): pl.pallas_call(functools.partial(update_kernel, weight), out_shape=(jax.S...  15.5 us
    pallas_call x1, Pallas kernels, per_device(): pl.pallas_call(functools.partial(prep_kernel, weight), out_shape=(jax.Sha...  5.52 us

profile of v3, /device:TPU:1, one launch (start us, length us, event | category | flops | bytes accessed | tf_op | source)
XLA Modules:
  0.0 90.5 jit_solution(9703901772345249339)
XLA Ops:
  3.2 0.0 copy-start
  3.2 5.5 %panels.1 = (f32[2,4,256,256]{3,2,1,0:T(8,128)S(1)}, f32[2,256,1024]{2,1,0:T(8,128)}, f32[2,512]{1,0:T(2,128)S(1)}) custom-call(s32[2]{0:T(128)} %sc.3, s32[8,8]{1,0:T(8,128)} %fill.3, f32[1024,1024]{1,0:T(8,128)} %front.1, f32[1024,1024]{1,0:T(8,128)} %front.1, f32[1024,1024]{1,0:T(8,128)} %front.1, f32[1024,1024]{1,0:T(8,128)} %front.1, ...), custom_call_target="tpu_custom_call" | custom-call | tf_op jit(solution)/shard_map/panels/pallas_call | solution.py:619
  8.8 0.0 copy-done
  8.8 66.2 %conditional.1 = (f32[2,4,256,256]{3,2,1,0:T(8,128)S(1)}, f32[2,2,4,64,256]{4,3,2,1,0:T(8,128)S(1)}, f32[16,2,1024]{2,1,0:T(2,128)S(1)}, f32[16,2,512]{2,1,0:T(2,128)S(1)}, f32[2,256,1024]{2,1,0:T(8,128)}) conditional(s32[]{:T(128)} %clamp.3, (f32[2,4,256,256]{3,2,1,0:T(8,128)S(1)}, f32[2,2,4,32,1024]{4,3,2,1,0:T(8,128)}, ...), branch_computations={%region_0.1_spmd, %region_1.2_spmd, %region_2.3_spmd, %region_3.4_... | conditional | bytes 40 | solution.py:647
  8.8 65.9 %exchange_2.1 = (f32[2,4,256,256]{3,2,1,0:T(8,128)S(1)}, f32[2,2,4,32,1024]{4,3,2,1,0:T(8,128)}, f32[2,2,4,64,256]{4,3,2,1,0:T(8,128)S(1)}, f32[16,2,1024]{2,1,0:T(2,128)S(1)}, f32[16,2,512]{2,1,0:T(2,128)S(1)}) custom-call(f32[2,4,256,256]{3,2,1,0:T(8,128)S(1)} %get-tuple-element.227.cin, ...), custom_call_target="tpu_custom_call", output_to_operand_aliasing={{0}: (0, {}), {1}: (1, {})} | custom-call | tf_op jit(solution)/shard_map/cond/branch_2_fun/exchange_2/pallas_call | solution.py:478
  75.0 15.5 %update.1 = (f32[1024,1024]{1,0:T(8,128)}, f32[32,1024]{1,0:T(8,128)}) custom-call(s32[2]{0:T(128)} %sc.3, s32[8,8]{1,0:T(8,128)} %fill.3, f32[1024,1024]{1,0:T(8,128)} %front.1, f32[8,128]{1,0:T(8,128)} %bitcast.53, f32[2,4,256,256]{3,2,1,0:T(8,128)S(1)} %get-tuple-element.366.cbuf, f32[2,256,1024]{2,1,0:T(8,128)} %get-tuple-element.367.rbuf, ...), custom_call_target="tpu_custom_call" | custom-call | tf_op jit(solution)/shard_map/update/pallas_call | solution.py:650
Async XLA Ops:
  3.2 5.5 %copy-start = (f32[2,16384]{1,0:T(2,128)S(1)}, f32[2,16384]{1,0:T(2,128)}, u32[]{:S(2)}) copy-start(f32[2,16384]{1,0:T(2,128)} %loads.1) | copy-start | bytes 393220

commit v4 on v3

--- a/solution.py
+++ b/solution.py
@@ -293,7 +293,7 @@
                     j = jnp.where(i == 1, 2, jnp.where(i == 2, 1, 3))
                     rsend(k, c, own, n, rs.at[k, j], xto(j))
 
-        @pl.when(t == 2)
+        @pl.when(t == 6)
         def _():
             for m in own_h:
                 m.start()

time: 91 us -> 85.1 us (0.935)
  Pallas kernels: 86.9 us -> 81.2 us
    pallas_call x1, Pallas kernels: 65.9 us -> 60 us  [comm(): pl.pallas_call(functools.partial(comm_kernel, r0), out_shape=(jax.ShapeDt...]
where the time goes in v4:
time: 85.1 us; the launch traced here: 84.8 us
  Pallas kernels  81.2 us (95%)
  between operations  3.25 us (4%)
    pallas_call x1, Pallas kernels, comm(): pl.pallas_call(functools.partial(comm_kernel, r0), out_shape=(jax.ShapeDt...  60 us
    pallas_call x1, Pallas kernels, per_device(): pl.pallas_call(functools.partial(update_kernel, weight), out_shape=(jax.S...  15.5 us
    pallas_call x1, Pallas kernels, per_device(): pl.pallas_call(functools.partial(prep_kernel, weight), out_shape=(jax.Sha...  5.71 us

profile of v4, /device:TPU:1, one launch (start us, length us, event | category | flops | bytes accessed | tf_op | source)
XLA Modules:
  0.0 84.8 jit_solution(15929355477200629702)
XLA Ops:
  3.2 0.0 copy-start
  3.2 5.7 %panels.1 = (f32[2,4,256,256]{3,2,1,0:T(8,128)S(1)}, f32[2,256,1024]{2,1,0:T(8,128)}, f32[2,512]{1,0:T(2,128)S(1)}) custom-call(s32[2]{0:T(128)} %sc.3, s32[8,8]{1,0:T(8,128)} %fill.3, f32[1024,1024]{1,0:T(8,128)} %front.1, f32[1024,1024]{1,0:T(8,128)} %front.1, f32[1024,1024]{1,0:T(8,128)} %front.1, f32[1024,1024]{1,0:T(8,128)} %front.1, ...), custom_call_target="tpu_custom_call" | custom-call | tf_op jit(solution)/shard_map/panels/pallas_call | solution.py:619
  8.9 0.0 copy-done
  9.0 60.3 %conditional.1 = (f32[2,4,256,256]{3,2,1,0:T(8,128)S(1)}, f32[2,2,4,64,256]{4,3,2,1,0:T(8,128)S(1)}, f32[16,2,1024]{2,1,0:T(2,128)S(1)}, f32[16,2,512]{2,1,0:T(2,128)S(1)}, f32[2,256,1024]{2,1,0:T(8,128)}) conditional(s32[]{:T(128)} %clamp.3, (f32[2,4,256,256]{3,2,1,0:T(8,128)S(1)}, f32[2,2,4,32,1024]{4,3,2,1,0:T(8,128)}, ...), branch_computations={%region_0.1_spmd, %region_1.2_spmd, %region_2.3_spmd, %region_3.4_... | conditional | bytes 40 | solution.py:647
  9.0 60.0 %exchange_4.1 = (f32[2,4,256,256]{3,2,1,0:T(8,128)S(1)}, f32[2,2,4,32,1024]{4,3,2,1,0:T(8,128)}, f32[2,2,4,64,256]{4,3,2,1,0:T(8,128)S(1)}, f32[16,2,1024]{2,1,0:T(2,128)S(1)}, f32[16,2,512]{2,1,0:T(2,128)S(1)}) custom-call(f32[2,4,256,256]{3,2,1,0:T(8,128)S(1)} %get-tuple-element.245.cin, ...), custom_call_target="tpu_custom_call", output_to_operand_aliasing={{0}: (0, {}), {1}: (1, {})} | custom-call | tf_op jit(solution)/shard_map/cond/branch_4_fun/exchange_4/pallas_call | solution.py:478
  69.2 15.5 %update.1 = (f32[1024,1024]{1,0:T(8,128)}, f32[32,1024]{1,0:T(8,128)}) custom-call(s32[2]{0:T(128)} %sc.3, s32[8,8]{1,0:T(8,128)} %fill.3, f32[1024,1024]{1,0:T(8,128)} %front.1, f32[8,128]{1,0:T(8,128)} %bitcast.53, f32[2,4,256,256]{3,2,1,0:T(8,128)S(1)} %get-tuple-element.366.cbuf, f32[2,256,1024]{2,1,0:T(8,128)} %get-tuple-element.367.rbuf, ...), custom_call_target="tpu_custom_call" | custom-call | tf_op jit(solution)/shard_map/update/pallas_call | solution.py:650
Async XLA Ops:
  3.2 5.7 %copy-start = (f32[2,16384]{1,0:T(2,128)S(1)}, f32[2,16384]{1,0:T(2,128)}, u32[]{:S(2)}) copy-start(f32[2,16384]{1,0:T(2,128)} %loads.1) | copy-start | bytes 393220
